TPU v7x, 256 devices: a whole 4x4x8 slice. The times are simulated.
256 devices in a mesh: dom: 16 (over x, y_lo, core), space: 16 (over y_hi, z).
Axes of the slice: x: 4, y: 4 (y_hi: 2, y_lo: 2; y = y_hi * 2 + y_lo), z: 8, core: 2. Of those that a mesh axis runs over, the one named last changes fastest.
Arguments:
- ancestor: int32 [64], replicated, may hold values from 0 to 63, as said below
- state: float32 [64, 3, 256, 2048], P('dom', None, 'space'), may hold values from -6 to 6
- jitter: float32 [64, 3, 256, 2048], P('dom', None, 'space'), may hold values from -4 to 4
- depth: float32 [256, 2048], P('space'), may hold values from 0.5 to 2
- coriolis: float32 [256, 2048], P('space'), may hold values from -1 to 1
- drag: float32 [256, 2048], P('space'), may hold values from 0.1 to 1
Outputs:
- forecast: float32 [64, 3, 256, 2048], P('dom', None, 'space')
Inputs may be any that keep to these rules, and one draw needn't show every extreme that they name: In-place replacement: every particle either keeps its slot (ancestor[j] = j) or is replaced by a survivor p with ancestor[p] = p and p != j; a survivor is the ancestor of at most two new particles. Among the particles k*4 to k*4 + 3, at most 2 are ancestors of a particle other than themselves, and in every draw some such block has exactly 2.
All inputs are finite; a program needn't handle non-finite values.
Results may differ from a plain program's by a relative error of at most 0.00007.
Values sent between devices are 32-bit elements; how exact they have to be, the bound alone decides.
No kernel may reach another device: no remote copies, remote signals or barrier semaphores. Data moves between devices by JAX's collectives and lax.ppermute only.
A program may use at most 128 MiB of HBM per device.

v0:
```python
import jax
import jax.numpy as jnp
from jax import lax
from jax.sharding import PartitionSpec as P

STEPS = 4
time_step = 0.3


def extended(cells, sides, width):
    for axis, dim in sides:
        count = lax.axis_size(axis)
        head = lax.slice_in_dim(cells, 0, width, axis=dim)
        tail = lax.slice_in_dim(cells, cells.shape[dim] - width, cells.shape[dim], axis=dim)
        cells = jnp.concatenate(
            [
                lax.ppermute(tail, axis, [(i, (i + 1) % count) for i in range(count)]),
                cells,
                lax.ppermute(head, axis, [((i + 1) % count, i) for i in range(count)]),
            ],
            axis=dim,
        )
    return cells


def diff_zero(values):
    padded = jnp.pad(values, [(0, 0)] * (values.ndim - 1) + [(1, 1)])
    return 0.5 * (padded[..., 2:] - padded[..., :-2])


def diff_edge(values):
    padded = jnp.pad(values, [(0, 0)] * (values.ndim - 1) + [(1, 1)], mode="edge")
    return 0.5 * (padded[..., 2:] - padded[..., :-2])


def local(ancestor, state, jitter, depth, coriolis, drag):
    members = state.shape[0]
    myself = lax.axis_index("dom")
    wanted = lax.dynamic_slice_in_dim(ancestor, myself * members, members)
    piece = lax.all_gather(state, "dom", axis=0, tiled=True)
    take_count = piece.shape[0]
    select = (wanted[:, None] == jnp.arange(take_count, dtype=jnp.int32)[None, :]).astype(
        jnp.float32
    )
    copied = jnp.einsum("jk,kfrc->jfrc", select, piece, precision=lax.Precision.HIGHEST)
    fields = copied + jitter
    height, across, along = (fields[:, 0], fields[:, 1], fields[:, 2])
    for count in range(STEPS):
        flux = depth * along
        padded = extended(flux, (("space", 1),), 1)
        height_new = height - time_step * (
            diff_zero(depth * across) + 0.5 * (padded[:, 2:] - padded[:, :-2])
        )
        rimmed = extended(height_new, (("space", 1),), 1)
        across_new = (across + time_step * (coriolis * along - diff_edge(height_new))) / (
            1.0 + time_step * drag
        )
        along_new = (
            along + time_step * (-coriolis * across - 0.5 * (rimmed[:, 2:] - rimmed[:, :-2]))
        ) / (1.0 + time_step * drag)
        height, across, along = (height_new, across_new, along_new)
    return jnp.stack([height, across, along], axis=1)


def solution(mesh):
    placed = (
        P(),
        P("dom", None, "space", None),
        P("dom", None, "space", None),
        P("space", None),
        P("space", None),
        P("space", None),
    )
    return jax.shard_map(
        local, mesh=mesh, in_specs=placed, out_specs=P("dom", None, "space", None), check_vma=False
    )
```

profile of v0, /device:TPU:2, one launch (start us, length us, event | category | flops | bytes accessed | tf_op | source)
XLA Modules:
  0.0 258.6 jit_solution(7539135098943396371)
XLA Ops:
  6.5 0.7 all-gather.2.cloned.1.call-update
  7.4 138.2 %all-gather.2.cloned.1.call-done = f32[64,3,16,2048]{3,2,1,0:T(8,128)} async-done(((f32[4,3,16,2048]{3,2,1,0:T(8,128)}), f32[64,3,16,2048]{3,2,1,0:T(8,128)}) %all-gather.2.cloned.1.call-update) | async-done | bytes 25165840 | tf_op jit(solution)/shard_map/all_gather | solution.py:40
  145.6 29.7 %fusion.2 = f32[4,3,16,2048]{3,0,2,1:T(4,128)S(1)} fusion(f32[64,3,16,2048]{3,2,1,0:T(8,128)} %all-gather.2.cloned.1.call-done, f32[4,3,16,2048]{3,2,1,0:T(8,128)S(1)} %copy-done.2, s32[4]{0:T(128)S(1)} %dynamic_slice.3), kind=kOutput, calls=%fused_computation.2 | convolution fusion | flops 302383360 | bytes 28311568 | tf_op jit(solution)/shard_map/jk,kfrc->jfrc/dot_general | solution.py:45
  175.5 5.8 %collective-permute-start = (f32[4,1,2048]{2,0,1:T(4,128)S(1)}, f32[4,1,2048]{2,0,1:T(4,128)S(1)}, u32[]{:S(2)}, u32[]{:S(2)}) collective-permute-start(f32[4,1,2048]{2,0,1:T(4,128)S(1)} %get-tuple-element.49), channel_id=1, source_target_pairs={{1,0},{2,1},{3,2},{4,3},{5,4},{6,5},{7,6},{8,7},{9,8},{10,9},{11,1... | collective-permute-start | bytes 98312 | tf_op jit(solution)/shard_map/ppermute | solution.py:19
  181.4 1.5 collective-permute-done
  183.0 5.9 %collective-permute-done.1 = f32[4,1,2048]{2,0,1:T(4,128)S(1)} collective-permute-done((f32[4,1,2048]{2,0,1:T(4,128)S(1)}, f32[4,1,2048]{2,0,1:T(4,128)S(1)}, u32[]{:S(2)}, u32[]{:S(2)}) %collective-permute-start.1) | collective-permute-done | bytes 32800 | tf_op jit(solution)/shard_map/ppermute | solution.py:17
  189.6 2.0 collective-permute-start.3
  191.7 1.8 collective-permute-done.2
  193.5 3.7 %collective-permute-done.3 = f32[4,1,2048]{2,0,1:T(4,128)S(1)} collective-permute-done((f32[4,1,2048]{2,0,1:T(4,128)S(1)}, f32[4,1,2048]{2,0,1:T(4,128)S(1)}, u32[]{:S(2)}, u32[]{:S(2)}) %collective-permute-start.3) | collective-permute-done | bytes 32800 | tf_op jit(solution)/shard_map/ppermute | solution.py:17
  197.2 1.0 broadcast_multiply_fusion.5
  198.3 2.0 collective-permute-start.5
  200.3 1.9 collective-permute-done.4
  202.2 3.7 %collective-permute-done.5 = f32[4,1,2048]{2,0,1:T(4,128)S(1)} collective-permute-done((f32[4,1,2048]{2,0,1:T(4,128)S(1)}, f32[4,1,2048]{2,0,1:T(4,128)S(1)}, u32[]{:S(2)}, u32[]{:S(2)}) %collective-permute-start.5) | collective-permute-done | bytes 32800 | tf_op jit(solution)/shard_map/ppermute | solution.py:17
  206.6 2.0 collective-permute-start.7
  208.7 1.8 collective-permute-done.6
  210.5 3.7 %collective-permute-done.7 = f32[4,1,2048]{2,0,1:T(4,128)S(1)} collective-permute-done((f32[4,1,2048]{2,0,1:T(4,128)S(1)}, f32[4,1,2048]{2,0,1:T(4,128)S(1)}, u32[]{:S(2)}, u32[]{:S(2)}) %collective-permute-start.7) | collective-permute-done | bytes 32800 | tf_op jit(solution)/shard_map/ppermute | solution.py:17
  214.2 1.0 broadcast_multiply_fusion.3
  215.3 2.0 collective-permute-start.9
  217.3 1.9 collective-permute-done.8
  219.2 3.7 %collective-permute-done.9 = f32[4,1,2048]{2,0,1:T(4,128)S(1)} collective-permute-done((f32[4,1,2048]{2,0,1:T(4,128)S(1)}, f32[4,1,2048]{2,0,1:T(4,128)S(1)}, u32[]{:S(2)}, u32[]{:S(2)}) %collective-permute-start.9) | collective-permute-done | bytes 32800 | tf_op jit(solution)/shard_map/ppermute | solution.py:17
  223.9 2.0 collective-permute-start.11
  225.9 1.8 collective-permute-done.10
  227.8 3.7 %collective-permute-done.11 = f32[4,1,2048]{2,0,1:T(4,128)S(1)} collective-permute-done((f32[4,1,2048]{2,0,1:T(4,128)S(1)}, f32[4,1,2048]{2,0,1:T(4,128)S(1)}, u32[]{:S(2)}, u32[]{:S(2)}) %collective-permute-start.11) | collective-permute-done | bytes 32800 | tf_op jit(solution)/shard_map/ppermute | solution.py:17
  231.5 1.0 broadcast_multiply_fusion.1
  232.5 2.0 collective-permute-start.13
  234.5 1.9 collective-permute-done.12
  236.4 3.7 %collective-permute-done.13 = f32[4,1,2048]{2,0,1:T(4,128)S(1)} collective-permute-done((f32[4,1,2048]{2,0,1:T(4,128)S(1)}, f32[4,1,2048]{2,0,1:T(4,128)S(1)}, u32[]{:S(2)}, u32[]{:S(2)}) %collective-permute-start.13) | collective-permute-done | bytes 32800 | tf_op jit(solution)/shard_map/ppermute | solution.py:17
  240.9 2.0 collective-permute-start.15
  243.0 1.8 collective-permute-done.14
  244.8 3.7 %collective-permute-done.15 = f32[4,1,2048]{2,0,1:T(4,128)S(1)} collective-permute-done((f32[4,1,2048]{2,0,1:T(4,128)S(1)}, f32[4,1,2048]{2,0,1:T(4,128)S(1)}, u32[]{:S(2)}, u32[]{:S(2)}) %collective-permute-start.15) | collective-permute-done | bytes 32800 | tf_op jit(solution)/shard_map/ppermute | solution.py:17
  248.5 0.8 fusion.69
  249.7 2.1 copy.12
  (40 shorter events, 4.4 us)
Async XLA Ops:
  6.5 0.7 copy-start.4
  6.5 139.0 %copy-start.2 = (f32[4,3,16,2048]{3,2,1,0:T(8,128)S(1)}, f32[4,3,16,2048]{3,2,1,0:T(8,128)}, u32[]{:S(2)}) copy-start(f32[4,3,16,2048]{3,2,1,0:T(8,128)} %param.8) | copy-start | bytes 4718596
  6.5 139.0 %all-gather.2.cloned.1.call-start = ((), (), s32[]{:S(2)}) async-start(), calls=%async_computation | async-start | bytes 26738688 | tf_op jit(solution)/shard_map/all_gather | solution.py:40
  7.4 167.9 %copy-start.1 = (f32[16,2048]{1,0:T(8,128)S(1)}, f32[16,2048]{1,0:T(8,128)}, u32[]{:S(2)}) copy-start(f32[16,2048]{1,0:T(8,128)} %param.9) | copy-start | bytes 393220
  175.3 6.1 %copy-start.3 = (f32[16,2048]{1,0:T(8,128)S(1)}, f32[16,2048]{1,0:T(8,128)}, u32[]{:S(2)}) copy-start(f32[16,2048]{1,0:T(8,128)} %param.11) | copy-start | bytes 393220
  175.3 6.1 %copy-start = (f32[16,2048]{1,0:T(8,128)S(1)}, f32[16,2048]{1,0:T(8,128)}, u32[]{:S(2)}) copy-start(f32[16,2048]{1,0:T(8,128)} %param.10) | copy-start | bytes 393220
  175.5 7.4 %collective-permute-start = (f32[4,1,2048]{2,0,1:T(4,128)S(1)}, f32[4,1,2048]{2,0,1:T(4,128)S(1)}, u32[]{:S(2)}, u32[]{:S(2)}) collective-permute-start(f32[4,1,2048]{2,0,1:T(4,128)S(1)} %get-tuple-element.49), channel_id=1, source_target_pairs={{1,0},{2,1},{3,2},{4,3},{5,4},{6,5},{7,6},{8,7},{9,8},{10,9},{11,1... | collective-permute-start | bytes 98312 | tf_op jit(solution)/shard_map/ppermute | solution.py:19
  181.4 7.5 %collective-permute-start.1 = (f32[4,1,2048]{2,0,1:T(4,128)S(1)}, f32[4,1,2048]{2,0,1:T(4,128)S(1)}, u32[]{:S(2)}, u32[]{:S(2)}) collective-permute-start(f32[4,1,2048]{2,0,1:T(4,128)S(1)} %get-tuple-element.50), channel_id=1, source_target_pairs={{0,1},{1,2},{2,3},{3,4},{4,5},{5,6},{6,7},{7,8},{8,9},{9,10},{10,1... | collective-permute-start | bytes 98312 | tf_op jit(solution)/shard_map/ppermute | solution.py:17
  189.5 4.0 %collective-permute-start.2 = (f32[4,1,2048]{2,0,1:T(4,128)S(1)}, f32[4,1,2048]{2,0,1:T(4,128)S(1)}, u32[]{:S(2)}, u32[]{:S(2)}) collective-permute-start(f32[4,1,2048]{2,0,1:T(4,128)S(1)} %get-tuple-element.47), channel_id=1, source_target_pairs={{1,0},{2,1},{3,2},{4,3},{5,4},{6,5},{7,6},{8,7},{9,8},{10,9},{11,1... | collective-permute-start | bytes 98312 | tf_op jit(solution)/shard_map/ppermute | solution.py:19
  189.6 7.6 %collective-permute-start.3 = (f32[4,1,2048]{2,0,1:T(4,128)S(1)}, f32[4,1,2048]{2,0,1:T(4,128)S(1)}, u32[]{:S(2)}, u32[]{:S(2)}) collective-permute-start(f32[4,1,2048]{2,0,1:T(4,128)S(1)} %get-tuple-element.48), channel_id=1, source_target_pairs={{0,1},{1,2},{2,3},{3,4},{4,5},{5,6},{6,7},{7,8},{8,9},{9,10},{10,1... | collective-permute-start | bytes 98312 | tf_op jit(solution)/shard_map/ppermute | solution.py:17
  198.2 4.0 %collective-permute-start.4 = (f32[4,1,2048]{2,0,1:T(4,128)S(1)}, f32[4,1,2048]{2,0,1:T(4,128)S(1)}, u32[]{:S(2)}, u32[]{:S(2)}) collective-permute-start(f32[4,1,2048]{2,0,1:T(4,128)S(1)} %get-tuple-element.45), channel_id=1, source_target_pairs={{1,0},{2,1},{3,2},{4,3},{5,4},{6,5},{7,6},{8,7},{9,8},{10,9},{11,1... | collective-permute-start | bytes 98312 | tf_op jit(solution)/shard_map/ppermute | solution.py:19
  198.3 7.6 %collective-permute-start.5 = (f32[4,1,2048]{2,0,1:T(4,128)S(1)}, f32[4,1,2048]{2,0,1:T(4,128)S(1)}, u32[]{:S(2)}, u32[]{:S(2)}) collective-permute-start(f32[4,1,2048]{2,0,1:T(4,128)S(1)} %get-tuple-element.46), channel_id=1, source_target_pairs={{0,1},{1,2},{2,3},{3,4},{4,5},{5,6},{6,7},{7,8},{8,9},{9,10},{10,1... | collective-permute-start | bytes 98312 | tf_op jit(solution)/shard_map/ppermute | solution.py:17
  206.5 4.0 %collective-permute-start.6 = (f32[4,1,2048]{2,0,1:T(4,128)S(1)}, f32[4,1,2048]{2,0,1:T(4,128)S(1)}, u32[]{:S(2)}, u32[]{:S(2)}) collective-permute-start(f32[4,1,2048]{2,0,1:T(4,128)S(1)} %get-tuple-element.41), channel_id=1, source_target_pairs={{1,0},{2,1},{3,2},{4,3},{5,4},{6,5},{7,6},{8,7},{9,8},{10,9},{11,1... | collective-permute-start | bytes 98312 | tf_op jit(solution)/shard_map/ppermute | solution.py:19
  206.6 7.6 %collective-permute-start.7 = (f32[4,1,2048]{2,0,1:T(4,128)S(1)}, f32[4,1,2048]{2,0,1:T(4,128)S(1)}, u32[]{:S(2)}, u32[]{:S(2)}) collective-permute-start(f32[4,1,2048]{2,0,1:T(4,128)S(1)} %get-tuple-element.42), channel_id=1, source_target_pairs={{0,1},{1,2},{2,3},{3,4},{4,5},{5,6},{6,7},{7,8},{8,9},{9,10},{10,1... | collective-permute-start | bytes 98312 | tf_op jit(solution)/shard_map/ppermute | solution.py:17
  215.2 4.0 %collective-permute-start.8 = (f32[4,1,2048]{2,0,1:T(4,128)S(1)}, f32[4,1,2048]{2,0,1:T(4,128)S(1)}, u32[]{:S(2)}, u32[]{:S(2)}) collective-permute-start(f32[4,1,2048]{2,0,1:T(4,128)S(1)} %get-tuple-element.39), channel_id=1, source_target_pairs={{1,0},{2,1},{3,2},{4,3},{5,4},{6,5},{7,6},{8,7},{9,8},{10,9},{11,1... | collective-permute-start | bytes 98312 | tf_op jit(solution)/shard_map/ppermute | solution.py:19
  215.3 7.6 %collective-permute-start.9 = (f32[4,1,2048]{2,0,1:T(4,128)S(1)}, f32[4,1,2048]{2,0,1:T(4,128)S(1)}, u32[]{:S(2)}, u32[]{:S(2)}) collective-permute-start(f32[4,1,2048]{2,0,1:T(4,128)S(1)} %get-tuple-element.40), channel_id=1, source_target_pairs={{0,1},{1,2},{2,3},{3,4},{4,5},{5,6},{6,7},{7,8},{8,9},{9,10},{10,1... | collective-permute-start | bytes 98312 | tf_op jit(solution)/shard_map/ppermute | solution.py:17
  223.5 4.2 %collective-permute-start.10 = (f32[4,1,2048]{2,0,1:T(4,128)S(1)}, f32[4,1,2048]{2,0,1:T(4,128)S(1)}, u32[]{:S(2)}, u32[]{:S(2)}) collective-permute-start(f32[4,1,2048]{2,0,1:T(4,128)S(1)} %get-tuple-element.35), channel_id=1, source_target_pairs={{1,0},{2,1},{3,2},{4,3},{5,4},{6,5},{7,6},{8,7},{9,8},{10,9},{11,1... | collective-permute-start | bytes 98312 | tf_op jit(solution)/shard_map/ppermute | solution.py:19
  223.9 7.6 %collective-permute-start.11 = (f32[4,1,2048]{2,0,1:T(4,128)S(1)}, f32[4,1,2048]{2,0,1:T(4,128)S(1)}, u32[]{:S(2)}, u32[]{:S(2)}) collective-permute-start(f32[4,1,2048]{2,0,1:T(4,128)S(1)} %get-tuple-element.36), channel_id=1, source_target_pairs={{0,1},{1,2},{2,3},{3,4},{4,5},{5,6},{6,7},{7,8},{8,9},{9,10},{10,1... | collective-permute-start | bytes 98312 | tf_op jit(solution)/shard_map/ppermute | solution.py:17
  232.4 4.0 %collective-permute-start.12 = (f32[4,1,2048]{2,0,1:T(4,128)S(1)}, f32[4,1,2048]{2,0,1:T(4,128)S(1)}, u32[]{:S(2)}, u32[]{:S(2)}) collective-permute-start(f32[4,1,2048]{2,0,1:T(4,128)S(1)} %get-tuple-element.33), channel_id=1, source_target_pairs={{1,0},{2,1},{3,2},{4,3},{5,4},{6,5},{7,6},{8,7},{9,8},{10,9},{11,1... | collective-permute-start | bytes 98312 | tf_op jit(solution)/shard_map/ppermute | solution.py:19
  232.5 7.6 %collective-permute-start.13 = (f32[4,1,2048]{2,0,1:T(4,128)S(1)}, f32[4,1,2048]{2,0,1:T(4,128)S(1)}, u32[]{:S(2)}, u32[]{:S(2)}) collective-permute-start(f32[4,1,2048]{2,0,1:T(4,128)S(1)} %get-tuple-element.34), channel_id=1, source_target_pairs={{0,1},{1,2},{2,3},{3,4},{4,5},{5,6},{6,7},{7,8},{8,9},{9,10},{10,1... | collective-permute-start | bytes 98312 | tf_op jit(solution)/shard_map/ppermute | solution.py:17
  240.8 4.0 %collective-permute-start.14 = (f32[4,1,2048]{2,0,1:T(4,128)S(1)}, f32[4,1,2048]{2,0,1:T(4,128)S(1)}, u32[]{:S(2)}, u32[]{:S(2)}) collective-permute-start(f32[4,1,2048]{2,0,1:T(4,128)S(1)} %get-tuple-element.29), channel_id=1, source_target_pairs={{1,0},{2,1},{3,2},{4,3},{5,4},{6,5},{7,6},{8,7},{9,8},{10,9},{11,1... | collective-permute-start | bytes 98312 | tf_op jit(solution)/shard_map/ppermute | solution.py:19
  240.9 7.6 %collective-permute-start.15 = (f32[4,1,2048]{2,0,1:T(4,128)S(1)}, f32[4,1,2048]{2,0,1:T(4,128)S(1)}, u32[]{:S(2)}, u32[]{:S(2)}) collective-permute-start(f32[4,1,2048]{2,0,1:T(4,128)S(1)} %get-tuple-element.30), channel_id=1, source_target_pairs={{0,1},{1,2},{2,3},{3,4},{4,5},{5,6},{6,7},{7,8},{8,9},{9,10},{10,1... | collective-permute-start | bytes 98312 | tf_op jit(solution)/shard_map/ppermute | solution.py:17
Sparse Core Ops, SparseCore 0:
  9.2 136.3 all-gather.1
where the time goes:
time: 259 us
  waiting for transfers between devices  185 us (71%)
  matrix products  29.7 us (11%)
  starting transfers between devices  20.7 us (8%)
  between operations  13.6 us (5%)
  other arithmetic  6.78 us (3%)
    all_gather x1, waiting for transfers between devices, local(): piece = lax.all_gather(state, 'dom', axis=0, tiled=True)  138 us
    ppermute x8, waiting for transfers between devices, extended(): lax.ppermute(tail, axis, [(i, (i + 1) % count) for i in range(count)])  31.9 us
    dot_general x1, matrix products, local(): jnp.einsum('jk,kfrc->jfrc', select, piece, precision=lax.Precision.HIGHEST)  29.7 us
    ppermute x8, waiting for transfers between devices, extended(): lax.ppermute(head, axis, [((i + 1) % count, i) for i in range(count)])  14.4 us
    ppermute x8, starting transfers between devices, extended(): lax.ppermute(tail, axis, [(i, (i + 1) % count) for i in range(count)])  14.1 us
    ppermute x8, starting transfers between devices, extended(): lax.ppermute(head, axis, [((i + 1) % count, i) for i in range(count)])  6.64 us
  transfers between devices with their start and end apart: 17, of which 17 were waited for; matrix products, arithmetic and copies ran while one was open for 0% of the time, Pallas kernels for 0%

commit v1 on v0

--- a/solution.py
+++ b/solution.py
@@ -37,7 +37,9 @@
     members = state.shape[0]
     myself = lax.axis_index("dom")
     wanted = lax.dynamic_slice_in_dim(ancestor, myself * members, members)
-    piece = lax.all_gather(state, "dom", axis=0, tiled=True)
+    piece = jnp.concatenate(
+        lax.all_to_all(jnp.stack([state] * lax.axis_size("dom")), "dom", 0, 0), axis=0
+    )
     take_count = piece.shape[0]
     select = (wanted[:, None] == jnp.arange(take_count, dtype=jnp.int32)[None, :]).astype(
         jnp.float32

time: 259 us -> 573 us (2.21)
  the two profiles are of different devices: /device:TPU:2 before, /device:TPU:12 now
where the time goes in v1:
time: 573 us; the launch traced here: 572 us
  waiting for transfers between devices  459 us (80%)
  local copies, waits for them, and re-layouts  64 us (11%)
  starting transfers between devices  28.7 us (5%)
  matrix products  13.3 us (2%)
  other arithmetic  6.78 us (1%)
    all_to_all x1, waiting for transfers between devices, local(): lax.all_to_all(jnp.stack([state] * lax.axis_size('dom')), 'dom', 0, 0)  412 us
    ppermute x8, waiting for transfers between devices, extended(): lax.ppermute(tail, axis, [(i, (i + 1) % count) for i in range(count)])  32.1 us
    reshape x1, local copies, waits for them, and re-layouts, local(): jnp.concatenate(lax.all_to_all(jnp.stack([state] * lax.axis_size('dom')),...  29 us
    all_to_all x1, local copies, waits for them, and re-layouts, local(): lax.all_to_all(jnp.stack([state] * lax.axis_size('dom')), 'dom', 0, 0)  21 us
    ppermute x8, waiting for transfers between devices, extended(): lax.ppermute(head, axis, [((i + 1) % count, i) for i in range(count)])  14.4 us
    ppermute x8, starting transfers between devices, extended(): lax.ppermute(tail, axis, [(i, (i + 1) % count) for i in range(count)])  14.1 us
    dot_general x1, matrix products, local(): jnp.einsum('jk,kfrc->jfrc', select, piece, precision=lax.Precision.HIGHEST)  13.3 us
  transfers between devices with their start and end apart: 17, of which 17 were waited for; matrix products, arithmetic and copies ran while one was open for 0% of the time, Pallas kernels for 0%

profile of v1, /device:TPU:12, one launch (start us, length us, event | category | flops | bytes accessed | tf_op | source)
XLA Modules:
  0.0 572.0 jit_solution(3457916224089330800)
XLA Ops:
  0.0 2.4 copy.10
  2.4 9.0 %stack.10 = f32[16,4,3,16,2048]{4,1,3,2,0:T(4,128)} broadcast(f32[4,3,16,2048]{3,0,2,1:T(4,128)S(1)} %copy.10), dimensions={1,2,3,4} | broadcast | bytes 26738688 | tf_op jit(solution)/shard_map/stack | solution.py:41
  11.5 7.6 %all-to-all-start = ((f32[16,4,3,16,2048]{4,1,3,2,0:T(4,128)}), f32[16,4,3,16,2048]{4,1,3,2,0:T(4,128)}, u32[]{:S(2)}, u32[]{:S(2)}) async-start(f32[16,4,3,16,2048]{4,1,3,2,0:T(4,128)} %stack.10), calls=%async_computation | async-start | bytes 50331648 | tf_op jit(solution)/shard_map/all_to_all | solution.py:41
  19.2 412.5 %all-to-all-done = f32[16,4,3,16,2048]{4,1,3,2,0:T(4,128)} async-done(((f32[16,4,3,16,2048]{4,1,3,2,0:T(4,128)}), f32[16,4,3,16,2048]{4,1,3,2,0:T(4,128)}, u32[]{:S(2)}, u32[]{:S(2)}) %all-to-all-start) | async-done | bytes 25165856 | tf_op jit(solution)/shard_map/all_to_all | solution.py:41
  431.6 21.0 %copy.11 = f32[16,4,3,16,2048]{4,1,0,3,2:T(4,128)} copy(f32[16,4,3,16,2048]{4,1,3,2,0:T(4,128)} %all-to-all-done) | data formatting | bytes 50331648 | tf_op jit(solution)/shard_map/all_to_all | solution.py:41
  452.7 29.0 %reshape.10 = f32[64,3,16,2048]{3,0,2,1:T(8,128)} reshape(f32[16,4,3,16,2048]{4,1,0,3,2:T(4,128)} %copy.11) | data formatting | bytes 50331648 | tf_op jit(solution)/shard_map/reshape | solution.py:40
  481.6 13.3 %convolution_add_fusion = f32[4,3,16,2048]{3,0,2,1:T(4,128)S(1)} fusion(f32[64,3,16,2048]{3,0,2,1:T(8,128)} %reshape.10, f32[4,3,16,2048]{3,2,1,0:T(8,128)S(1)} %copy-done.2, s32[4]{0:T(128)S(1)} %dynamic_slice.3), kind=kOutput, calls=%fused_computation | convolution fusion | flops 302383360 | bytes 28311568 | tf_op jit(solution)/shard_map/jk,kfrc->jfrc/dot_general | solution.py:47
  495.3 6.2 %collective-permute-start = (f32[4,1,2048]{2,0,1:T(4,128)S(1)}, f32[4,1,2048]{2,0,1:T(4,128)S(1)}, u32[]{:S(2)}, u32[]{:S(2)}) collective-permute-start(f32[4,1,2048]{2,0,1:T(4,128)S(1)} %get-tuple-element.49), channel_id=1, source_target_pairs={{1,0},{2,1},{3,2},{4,3},{5,4},{6,5},{7,6},{8,7},{9,8},{10,9},{11,1... | collective-permute-start | bytes 98312 | tf_op jit(solution)/shard_map/ppermute | solution.py:19
  501.6 1.5 collective-permute-done
  503.1 5.9 %collective-permute-done.1 = f32[4,1,2048]{2,0,1:T(4,128)S(1)} collective-permute-done((f32[4,1,2048]{2,0,1:T(4,128)S(1)}, f32[4,1,2048]{2,0,1:T(4,128)S(1)}, u32[]{:S(2)}, u32[]{:S(2)}) %collective-permute-start.1) | collective-permute-done | bytes 32800 | tf_op jit(solution)/shard_map/ppermute | solution.py:17
  509.7 2.0 collective-permute-start.3
  511.8 1.8 collective-permute-done.2
  513.6 3.7 collective-permute-done.3
  518.6 2.0 collective-permute-start.5
  520.6 1.9 collective-permute-done.4
  522.5 3.7 collective-permute-done.5
  526.9 2.0 collective-permute-start.7
  529.0 1.8 collective-permute-done.6
  530.8 3.7 collective-permute-done.7
  535.6 2.0 collective-permute-start.9
  537.6 1.9 collective-permute-done.8
  539.5 3.7 collective-permute-done.9
  543.9 2.0 collective-permute-start.11
  546.0 1.8 collective-permute-done.10
  547.8 3.7 collective-permute-done.11
  552.6 2.0 collective-permute-start.13
  554.6 1.9 collective-permute-done.12
  556.5 3.7 collective-permute-done.13
  560.9 2.0 collective-permute-start.15
  563.0 1.8 collective-permute-done.14
  564.8 3.9 collective-permute-done.15
  570.0 2.1 copy.13
  (43 shorter events, 8.0 us)
Async XLA Ops:
  11.5 7.6 %copy-start.4 = (s32[64]{0:T(128)S(1)}, s32[64]{0:T(128)}, u32[]{:S(2)}) copy-start(s32[64]{0:T(128)} %param.6) | copy-start | bytes 772
  11.5 420.2 %all-to-all-start = ((f32[16,4,3,16,2048]{4,1,3,2,0:T(4,128)}), f32[16,4,3,16,2048]{4,1,3,2,0:T(4,128)}, u32[]{:S(2)}, u32[]{:S(2)}) async-start(f32[16,4,3,16,2048]{4,1,3,2,0:T(4,128)} %stack.10), calls=%async_computation | async-start | bytes 50331648 | tf_op jit(solution)/shard_map/all_to_all | solution.py:41
  452.7 29.0 %copy-start.2 = (f32[4,3,16,2048]{3,2,1,0:T(8,128)S(1)}, f32[4,3,16,2048]{3,2,1,0:T(8,128)}, u32[]{:S(2)}) copy-start(f32[4,3,16,2048]{3,2,1,0:T(8,128)} %param.8) | copy-start | bytes 4718596
  481.6 13.3 %copy-start.1 = (f32[16,2048]{1,0:T(8,128)S(1)}, f32[16,2048]{1,0:T(8,128)}, u32[]{:S(2)}) copy-start(f32[16,2048]{1,0:T(8,128)} %param.9) | copy-start | bytes 393220
  495.0 6.5 %copy-start.3 = (f32[16,2048]{1,0:T(8,128)S(1)}, f32[16,2048]{1,0:T(8,128)}, u32[]{:S(2)}) copy-start(f32[16,2048]{1,0:T(8,128)} %param.11) | copy-start | bytes 393220
  495.0 6.5 %copy-start = (f32[16,2048]{1,0:T(8,128)S(1)}, f32[16,2048]{1,0:T(8,128)}, u32[]{:S(2)}) copy-start(f32[16,2048]{1,0:T(8,128)} %param.10) | copy-start | bytes 393220
  495.3 7.8 %collective-permute-start = (f32[4,1,2048]{2,0,1:T(4,128)S(1)}, f32[4,1,2048]{2,0,1:T(4,128)S(1)}, u32[]{:S(2)}, u32[]{:S(2)}) collective-permute-start(f32[4,1,2048]{2,0,1:T(4,128)S(1)} %get-tuple-element.49), channel_id=1, source_target_pairs={{1,0},{2,1},{3,2},{4,3},{5,4},{6,5},{7,6},{8,7},{9,8},{10,9},{11,1... | collective-permute-start | bytes 98312 | tf_op jit(solution)/shard_map/ppermute | solution.py:19
  501.5 7.5 %collective-permute-start.1 = (f32[4,1,2048]{2,0,1:T(4,128)S(1)}, f32[4,1,2048]{2,0,1:T(4,128)S(1)}, u32[]{:S(2)}, u32[]{:S(2)}) collective-permute-start(f32[4,1,2048]{2,0,1:T(4,128)S(1)} %get-tuple-element.50), channel_id=1, source_target_pairs={{0,1},{1,2},{2,3},{3,4},{4,5},{5,6},{6,7},{7,8},{8,9},{9,10},{10,1... | collective-permute-start | bytes 98312 | tf_op jit(solution)/shard_map/ppermute | solution.py:17
  509.7 4.0 collective-permute-start.2
  509.7 7.6 %collective-permute-start.3 = (f32[4,1,2048]{2,0,1:T(4,128)S(1)}, f32[4,1,2048]{2,0,1:T(4,128)S(1)}, u32[]{:S(2)}, u32[]{:S(2)}) collective-permute-start(f32[4,1,2048]{2,0,1:T(4,128)S(1)} %get-tuple-element.48), channel_id=1, source_target_pairs={{0,1},{1,2},{2,3},{3,4},{4,5},{5,6},{6,7},{7,8},{8,9},{9,10},{10,1... | collective-permute-start | bytes 98312 | tf_op jit(solution)/shard_map/ppermute | solution.py:17
  518.3 4.2 collective-permute-start.4
  518.6 7.6 %collective-permute-start.5 = (f32[4,1,2048]{2,0,1:T(4,128)S(1)}, f32[4,1,2048]{2,0,1:T(4,128)S(1)}, u32[]{:S(2)}, u32[]{:S(2)}) collective-permute-start(f32[4,1,2048]{2,0,1:T(4,128)S(1)} %get-tuple-element.46), channel_id=1, source_target_pairs={{0,1},{1,2},{2,3},{3,4},{4,5},{5,6},{6,7},{7,8},{8,9},{9,10},{10,1... | collective-permute-start | bytes 98312 | tf_op jit(solution)/shard_map/ppermute | solution.py:17
  526.8 4.0 collective-permute-start.6
  526.9 7.6 %collective-permute-start.7 = (f32[4,1,2048]{2,0,1:T(4,128)S(1)}, f32[4,1,2048]{2,0,1:T(4,128)S(1)}, u32[]{:S(2)}, u32[]{:S(2)}) collective-permute-start(f32[4,1,2048]{2,0,1:T(4,128)S(1)} %get-tuple-element.42), channel_id=1, source_target_pairs={{0,1},{1,2},{2,3},{3,4},{4,5},{5,6},{6,7},{7,8},{8,9},{9,10},{10,1... | collective-permute-start | bytes 98312 | tf_op jit(solution)/shard_map/ppermute | solution.py:17
  535.5 4.0 collective-permute-start.8
  535.6 7.6 %collective-permute-start.9 = (f32[4,1,2048]{2,0,1:T(4,128)S(1)}, f32[4,1,2048]{2,0,1:T(4,128)S(1)}, u32[]{:S(2)}, u32[]{:S(2)}) collective-permute-start(f32[4,1,2048]{2,0,1:T(4,128)S(1)} %get-tuple-element.40), channel_id=1, source_target_pairs={{0,1},{1,2},{2,3},{3,4},{4,5},{5,6},{6,7},{7,8},{8,9},{9,10},{10,1... | collective-permute-start | bytes 98312 | tf_op jit(solution)/shard_map/ppermute | solution.py:17
  543.8 4.0 collective-permute-start.10
  543.9 7.6 %collective-permute-start.11 = (f32[4,1,2048]{2,0,1:T(4,128)S(1)}, f32[4,1,2048]{2,0,1:T(4,128)S(1)}, u32[]{:S(2)}, u32[]{:S(2)}) collective-permute-start(f32[4,1,2048]{2,0,1:T(4,128)S(1)} %get-tuple-element.36), channel_id=1, source_target_pairs={{0,1},{1,2},{2,3},{3,4},{4,5},{5,6},{6,7},{7,8},{8,9},{9,10},{10,1... | collective-permute-start | bytes 98312 | tf_op jit(solution)/shard_map/ppermute | solution.py:17
  552.5 4.0 collective-permute-start.12
  552.6 7.6 %collective-permute-start.13 = (f32[4,1,2048]{2,0,1:T(4,128)S(1)}, f32[4,1,2048]{2,0,1:T(4,128)S(1)}, u32[]{:S(2)}, u32[]{:S(2)}) collective-permute-start(f32[4,1,2048]{2,0,1:T(4,128)S(1)} %get-tuple-element.34), channel_id=1, source_target_pairs={{0,1},{1,2},{2,3},{3,4},{4,5},{5,6},{6,7},{7,8},{8,9},{9,10},{10,1... | collective-permute-start | bytes 98312 | tf_op jit(solution)/shard_map/ppermute | solution.py:17
  560.8 4.0 collective-permute-start.14
  560.9 7.8 %collective-permute-start.15 = (f32[4,1,2048]{2,0,1:T(4,128)S(1)}, f32[4,1,2048]{2,0,1:T(4,128)S(1)}, u32[]{:S(2)}, u32[]{:S(2)}) collective-permute-start(f32[4,1,2048]{2,0,1:T(4,128)S(1)} %get-tuple-element.30), channel_id=1, source_target_pairs={{0,1},{1,2},{2,3},{3,4},{4,5},{5,6},{6,7},{7,8},{8,9},{9,10},{10,1... | collective-permute-start | bytes 98312 | tf_op jit(solution)/shard_map/ppermute | solution.py:17
